TPU v7x, 256 devices: a whole 4x4x8 slice. The times are simulated.
256 devices in a mesh: ctx: 4 (over y), row: 4 (over x_hi, core), col: 16 (over x_lo, z).
Axes of the slice: x: 4 (x_hi: 2, x_lo: 2; x = x_hi * 2 + x_lo), y: 4, z: 8, core: 2. Of those that a mesh axis runs over, the one named last changes fastest.
Arguments:
- events: bfloat16 [8192, 4096], P(('ctx', 'row'), 'col'), may hold values from -120 to 120
- domain_ids: int32 [8192], P(('ctx', 'row')), may hold values from 0 to 3
- block_order: int32 [4], replicated, may hold values from 0 to 3, each once
- query_weight: bfloat16 [4096, 4096], P('row', 'col'), may hold values from -0.09375 to 0.09375
- keyval_weight: bfloat16 [4096, 8, 2, 128], P('row'), may hold values from -0.09375 to 0.09375
- head_bias: float32 [32], P('col'), may hold values from -1.5 to 1.5
- out_weight: bfloat16 [4096, 4096], P('row', 'col'), may hold values from -0.09375 to 0.09375
Outputs:
- mixed: bfloat16 [8192, 4096], P(('ctx', 'row'), 'col')
Inputs may be any that keep to these rules, and one draw needn't show every extreme that they name: `block_order`: each index of ctx holds 2048 consecutive events of one block; every place 0 to 3 is named once.
All inputs are finite; a program needn't handle non-finite values.
Results may differ from a plain program's by a relative error of at most 0.0075.
Values may be sent and summed in bfloat16 or wider, within the bound.
No kernel may reach another device: no remote copies, remote signals or barrier semaphores. Data moves between devices by JAX's collectives and lax.ppermute only.
A program may use at most 128 MiB of HBM per device.

v0:
```python
import math
import jax
import jax.numpy as jnp
from jax import lax
from jax.sharding import Mesh
from jax.sharding import PartitionSpec as P

H = 32
KV = 8
HD = 128
COL = ("col_0", "col_1")
norm_eps = 1e-06
block_rows = 512


def in_order(blocks, dim):
    dims = list(blocks.shape[1:])
    dims[dim] *= blocks.shape[0]
    return jnp.moveaxis(blocks, 0, dim).reshape(dims)


def gather_in_order(shard, axes, sequence):
    blocks = shard[None]
    for k in sequence:
        blocks = lax.all_gather(blocks, axes[k], axis=0, tiled=True)
    current = [lax.axis_size(axes[k]) for k in reversed(sequence)]
    blocks = blocks.reshape(*current, *shard.shape)
    turned = sorted(range(len(sequence)), key=lambda place: sequence[len(sequence) - 1 - place])
    return blocks.transpose(*turned, *range(len(sequence), blocks.ndim)).reshape(-1, *shard.shape)


def gather_axes(shard, axes, sequence, dim):
    return in_order(gather_in_order(shard, axes, sequence), dim)


def side_by_side(arrays, axis, dim, along):
    both = jnp.concatenate(arrays, axis=along)
    filled, at, outs = (lax.all_gather(both, axis, axis=dim, tiled=True), 0, [])
    for a in arrays:
        outs.append(lax.slice_in_dim(filled, at, at + a.shape[along], axis=along))
        at += a.shape[along]
    return tuple(outs)


def sent_to_all(shard, axis):
    devices = lax.axis_size(axis)
    return lax.all_to_all(
        jnp.broadcast_to(shard[None], (devices, *shard.shape)), axis, 0, 0, tiled=True
    )


def collect(shard, axis, dim):
    return in_order(sent_to_all(shard, axis), dim)


def block_place(storage, group_rows, block_order):
    block_index = storage // group_rows
    choices_row = jnp.arange(block_order.shape[0], dtype=jnp.int32)
    looked_up = jnp.sum(
        jnp.where(block_index[:, None] == choices_row[None, :], block_order[None, :], 0), axis=1
    )
    return looked_up * group_rows + storage % group_rows


def shards(events, domain_ids, block_order, query_weight, keyval_weight, head_bias, out_weight):
    row_count = events.shape[0]
    head_count = head_bias.shape[0]
    group_size = H // KV
    pair_heads = max(1, head_count // group_size)
    group_heads = head_count // pair_heads
    group_rows = row_count * lax.axis_size("row")
    scale_factor = 1.0 / math.sqrt(HD)
    whole = gather_axes(events, COL, (0, 1), 1)
    wide_events = whole.astype(jnp.float32)
    normed = (
        wide_events
        * lax.rsqrt(jnp.mean(wide_events * wide_events, axis=1, keepdims=True) + norm_eps)
    ).astype(jnp.bfloat16)
    pair_start = lax.axis_index(COL) * head_count // group_size
    pair_weight = lax.dynamic_slice_in_dim(keyval_weight, pair_start, pair_heads, 1)
    pair_weight = pair_weight.reshape(keyval_weight.shape[0], pair_heads * 2 * HD)
    portions = side_by_side((query_weight, pair_weight), "row", 0, 1)
    columns = normed
    query_sums = jnp.dot(columns, portions[0], preferred_element_type=jnp.float32)
    pair_sums = jnp.dot(columns, portions[1], preferred_element_type=jnp.float32)
    queries = query_sums.astype(jnp.bfloat16).reshape(row_count, pair_heads, group_heads, HD)
    keyvals = pair_sums.astype(jnp.bfloat16).reshape(row_count, pair_heads, 2, HD)
    first_row = (lax.axis_index("ctx") * lax.axis_size("row") + lax.axis_index("row")) * row_count
    query_place = block_place(
        first_row + jnp.arange(row_count, dtype=jnp.int32), group_rows, block_order
    )
    inv_count = lax.rsqrt((query_place + 1).astype(jnp.float32))
    head_terms = head_bias.reshape(pair_heads, group_heads)

    def compute_block(running, kv_block, domain_block, key_place):
        scores = (
            jnp.einsum(
                "qkgd,nkd->kgqn", queries, kv_block[:, :, 0, :], preferred_element_type=jnp.float32
            )
            * scale_factor
        )
        same_domain = (domain_ids[:, None] == domain_block[None, :]).astype(jnp.float32)
        scores = scores + head_terms[:, :, None, None] * same_domain[None, None, :, :]
        visible = key_place[None, :] <= query_place[:, None]
        weights = jnp.where(
            visible[None, None, :, :], jax.nn.silu(scores) * inv_count[None, None, :, None], 0.0
        ).astype(jnp.bfloat16)
        return running + jnp.einsum(
            "kgqn,nkd->qkgd", weights, kv_block[:, :, 1, :], preferred_element_type=jnp.float32
        )

    def update(running, kv_block, domain_block, block_first):
        key_place = block_place(
            block_first + jnp.arange(kv_block.shape[0], dtype=jnp.int32), group_rows, block_order
        )
        return compute_block(running, kv_block, domain_block, key_place)

    empty_sums = jnp.zeros((row_count, pair_heads, group_heads, HD), jnp.float32)
    totals = empty_sums
    kv_part = lax.all_gather(keyvals, ("ctx", "row"), axis=0, tiled=True)
    domain_part = lax.all_gather(domain_ids, ("ctx", "row"), axis=0, tiled=True)
    length_rows = kv_part.shape[0]
    number = length_rows // block_rows
    kv_blocks = kv_part.reshape((number, block_rows) + kv_part.shape[1:])
    domain_blocks = domain_part.reshape(number, block_rows)
    firsts = block_rows * jnp.arange(number, dtype=jnp.int32)

    def scan_step(running, block_item):
        return (update(running, block_item[0], block_item[1], block_item[2]), None)

    totals, unused = lax.scan(scan_step, totals, (kv_blocks, domain_blocks, firsts))
    attended = totals
    attended = attended.astype(jnp.bfloat16).reshape(row_count, head_count * HD)
    all_heads = lax.all_gather(attended, COL, axis=1, tiled=True)
    columns = all_heads
    out_sums = jnp.dot(columns, collect(out_weight, "row", 0), preferred_element_type=jnp.float32)
    return out_sums.astype(jnp.bfloat16)


def solution(mesh):
    split = Mesh(
        mesh.devices.reshape(mesh.shape["ctx"], mesh.shape["row"], 2, 8),
        ("ctx", "row", "col_0", "col_1"),
    )
    return jax.shard_map(
        shards,
        mesh=split,
        in_specs=(
            P(("ctx", "row"), COL),
            P(("ctx", "row")),
            P(),
            P("row", COL),
            P("row", None, None, None),
            P(COL),
            P("row", COL),
        ),
        out_specs=P(("ctx", "row"), COL),
        check_vma=False,
    )
```

profile of v0, /device:TPU:8, one launch (start us, length us, event | category | flops | bytes accessed | tf_op | source)
XLA Modules:
  0.0 338.7 jit_solution(12113207221270040131)
XLA Ops:
  6.5 10.4 %all-gather = bf16[1024,256]{1,0:T(8,128)(2,1)} all-gather(bf16[512,256]{1,0:T(8,128)(2,1)} %param.9), channel_id=2, replica_groups=mesh['ctx'=4,'row'=4,'col_0'=2,'col_1'=8] {'col_0'}, dimensions={0}, use_global_device_ids=true | all-gather | bytes 786432 | tf_op jit(solution)/shard_map/all_gather | solution.py:25
  17.0 1.4 constant_dynamic-slice_fusion.1
  18.6 2.2 pad_maximum_fusion
  20.8 53.7 %all-gather.7.cloned.1.call-done = bf16[16,512,256]{2,1,0:T(8,128)(2,1)} async-done(((bf16[2,512,256]{2,1,0:T(8,128)(2,1)}), bf16[16,512,256]{2,1,0:T(8,128)(2,1)}) %all-gather.7.cloned.1.call-update) | async-done | bytes 4194320 | tf_op jit(solution)/shard_map/all_gather | solution.py:25
  74.5 3.1 convert_bitcast_fusion
  77.6 3.8 %copy.33 = f32[2,8,512,256]{3,2,1,0:T(8,128)} copy(f32[2,8,512,256]{3,2,0,1:T(8,128)S(1)} %convert_bitcast_fusion) | data formatting | bytes 16777216 | tf_op jit(solution)/shard_map/convert_element_type | solution.py:74
  81.4 9.4 %copy.34 = f32[512,16,256]{0,2,1:T(8,128)} copy(f32[512,16,256]{2,0,1:T(8,128)} %bitcast.98) | data formatting | bytes 16777216 | tf_op jit(solution)/shard_map/convert_element_type | solution.py:74
  90.8 3.1 fusion.20
  93.9 6.6 %fusion.21 = bf16[512,4096]{0,1:T(8,128)(2,1)} fusion(f32[512,16,256]{0,2,1:T(8,128)} %copy.34, f32[512]{0:T(512)S(1)} %add_rsqrt_fusion), kind=kLoop, calls=%fused_computation.40 | loop fusion | flops 4194304 | bytes 12584960 | tf_op jit(solution)/shard_map/convert_element_type | solution.py:78
  100.5 15.5 %all-gather.9.cloned.1.call-done = bf16[4096,512]{1,0:T(8,128)(2,1)} async-done(((bf16[1024,512]{1,0:T(8,128)(2,1)}), bf16[4096,512]{1,0:T(8,128)(2,1)}) %all-gather.9.cloned.1.call-update) | async-done | bytes 4194320 | tf_op jit(solution)/shard_map/all_gather | solution.py:38
  116.0 4.2 %fusion.26 = bf16[512,256]{0,1:T(8,128)(2,1)S(1)} fusion(bf16[512,4096]{0,1:T(8,128)(2,1)} %fusion.21, bf16[4096,512]{1,0:T(8,128)(2,1)} %all-gather.9.cloned.1.call-done), kind=kOutput, calls=%fused_computation.45 | convolution fusion | flops 1073872896 | bytes 6553600 | tf_op jit(solution)/shard_map/dot_general | solution.py:85
  121.1 19.7 %all-gather.1 = s32[16,1,512]{2,1,0:T(1,128)S(1)} all-gather(s32[1,1,512]{2,1,0:T(1,128)S(1)} %bitcast.109), channel_id=1, replica_groups=mesh['ctx'=4,'row'=4,'col_0'=2,'col_1'=8] {'ctx','row'}, dimensions={0}, use_global_device_ids=true | all-gather | bytes 34816 | tf_op jit(solution)/shard_map/all_gather | solution.py:121
  140.9 4.2 %fusion.29 = bf16[512,256]{0,1:T(8,128)(2,1)S(1)} fusion(bf16[512,4096]{0,1:T(8,128)(2,1)} %fusion.21, bf16[4096,512]{1,0:T(8,128)(2,1)} %all-gather.9.cloned.1.call-done), kind=kOutput, calls=%fused_computation.46 | convolution fusion | flops 1073872896 | bytes 6553600 | tf_op jit(solution)/shard_map/dot_general | solution.py:84
  145.3 34.0 %all-gather.11.cloned.1.call-done = bf16[8192,1,2,128]{3,0,2,1:T(8,128)(2,1)} async-done(((bf16[512,1,2,128]{3,0,2,1:T(8,128)(2,1)}), bf16[8192,1,2,128]{3,0,2,1:T(8,128)(2,1)}) %all-gather.11.cloned.1.call-update) | async-done | bytes 4194320 | tf_op jit(solution)/shard_map/all_gather | solution.py:120
  179.2 72.2 %while.13 = (s32[]{:T(128)}, f32[512,1,2,128]{0,3,2,1:T(8,128)S(1)}, bf16[16,512,1,2,128]{4,1,0,3,2:T(8,128)(2,1)}, s32[16]{0:T(128)S(1)}, s32[4]{0:T(128)S(1)},...) while((s32[]{:T(128)}, ...), condition=%wide.region_4.5_spmd.clone, body=%wide.region_2.4_spmd.clone.sunk | while | flops 274747904 | bytes 4743363 | solution.py:131
  182.5 1.2 fusion.46
  191.6 1.2 fusion.46
  196.1 1.2 fusion.46
  205.1 1.2 fusion.46
  209.6 1.2 fusion.46
  214.1 1.2 fusion.46
  252.4 69.7 %all_to_all.5 = bf16[4,1024,256]{2,1,0:T(8,128)(2,1)S(1)} all-to-all(bf16[4,1024,256]{2,1,0:T(8,128)(2,1)S(1)} %broadcast_in_dim.74), channel_id=1, replica_groups=mesh['ctx'=4,'row'=4,'col_0'=2,'col_1'=8] {'row'}, dimensions={0} | all-to-all | bytes 4194304 | tf_op jit(solution)/shard_map/all_to_all | solution.py:47
  322.0 6.0 %all-gather.13.cloned.1.call-done = bf16[512,4096]{0,1:T(8,128)(2,1)} async-done(((bf16[512,256]{0,1:T(8,128)(2,1)}), bf16[512,4096]{0,1:T(8,128)(2,1)}) %all-gather.13.cloned.1.call-update) | async-done | bytes 4194320 | tf_op jit(solution)/shard_map/all_gather | solution.py:134
  328.0 4.2 %convolution_convert_fusion = bf16[512,256]{1,0:T(8,128)(2,1)} fusion(bf16[512,4096]{0,1:T(8,128)(2,1)} %all-gather.13.cloned.1.call-done, bf16[4096,256]{1,0:T(8,128)(2,1)S(1)} %bitcast.100), kind=kOutput, calls=%fused_computation.47 | convolution fusion | flops 1073872896 | bytes 6553600 | tf_op jit(solution)/shard_map/dot_general | solution.py:136
  (150 shorter events, 66.3 us)
Async XLA Ops:
  6.5 67.9 %all-gather.7.cloned.1.call-start = ((), (), s32[]{:S(2)}) async-start(), calls=%async_computation.1 | async-start | bytes 4718592 | tf_op jit(solution)/shard_map/all_gather | solution.py:25
  17.0 99.0 %all-gather.9.cloned.1.call-start = ((), (), s32[]{:S(2)}) async-start(), calls=%async_computation.2 | async-start | bytes 5242880 | tf_op jit(solution)/shard_map/all_gather | solution.py:38
  20.8 158.5 %all-gather.11.cloned.1.call-start = ((), (), s32[]{:S(2)}) async-start(), calls=%async_computation.3 | async-start | bytes 4456448 | tf_op jit(solution)/shard_map/all_gather | solution.py:120
  100.5 20.6 %copy-start.1 = (s32[512]{0:T(512)S(1)}, s32[512]{0:T(512)}, u32[]{:S(2)}) copy-start(s32[512]{0:T(512)} %param.10) | copy-start | bytes 6148
  100.5 40.3 %copy-start.2 = (s32[4]{0:T(128)S(1)}, s32[4]{0:T(128)}, u32[]{:S(2)}) copy-start(s32[4]{0:T(128)} %param.11) | copy-start | bytes 52
  121.0 207.0 %all-gather.13.cloned.1.call-start = ((), (), s32[]{:S(2)}) async-start(), calls=%async_computation.4 | async-start | bytes 4456448 | tf_op jit(solution)/shard_map/all_gather | solution.py:134
  140.9 38.4 %copy-start.3 = (f32[2]{0:T(128)S(1)}, f32[2]{0:T(128)}, u32[]{:S(2)}) copy-start(f32[2]{0:T(128)} %param.14) | copy-start | bytes 28
  179.2 73.0 %copy-start = (bf16[1024,256]{1,0:T(8,128)(2,1)S(1)}, bf16[1024,256]{1,0:T(8,128)(2,1)}, u32[]{:S(2)}) copy-start(bf16[1024,256]{1,0:T(8,128)(2,1)} %param.15) | copy-start | bytes 1572868
Sparse Core Ops, SparseCore 0:
  17.1 57.3 all-gather.6
  76.3 39.6 all-gather.8
  121.1 58.0 all-gather.10
  252.3 75.6 all-gather.12
where the time goes:
time: 340 us; the launch traced here: 339 us
  waiting for transfers between devices  109 us (32%)
  blocking collectives  99.8 us (29%)
  other arithmetic  42.6 us (13%)
  local copies, waits for them, and re-layouts  41.1 us (12%)
  matrix products  31.9 us (9%)
  between operations  13.3 us (4%)
    all_to_all x1, blocking collectives, sent_to_all(): lax.all_to_all(jnp.broadcast_to(shard[None], (devices, *shard.shape)), ax...  69.7 us
    all_gather x1, waiting for transfers between devices, gather_in_order(): blocks = lax.all_gather(blocks, axes[k], axis=0, tiled=True)  53.7 us
    all_gather x1, waiting for transfers between devices, shards(): kv_part = lax.all_gather(keyvals, ('ctx', 'row'), axis=0, tiled=True)  34 us
    all_gather x1, blocking collectives, shards(): domain_part = lax.all_gather(domain_ids, ('ctx', 'row'), axis=0, tiled=True)  19.7 us
    dot_general x16, matrix products, compute_block(): jnp.einsum('kgqn,nkd->qkgd', weights, kv_block[:, :, 1, :], preferred_ele...  19.3 us
    squeeze x16, local copies, waits for them, and re-layouts, shards(): lax.scan(scan_step, totals, (kv_blocks, domain_blocks, firsts))  15.6 us
    all_gather x1, waiting for transfers between devices, side_by_side(): filled, at, outs = (lax.all_gather(both, axis, axis=dim, tiled=True), 0, [])  15.5 us
    convert_element_type x2, local copies, waits for them, and re-layouts, shards(): wide_events = whole.astype(jnp.float32)  13.2 us
  transfers between devices with their start and end apart: 4, of which 4 were waited for; matrix products, arithmetic and copies ran while one was open for 10% of the time, Pallas kernels for 0%

commit v1 on v0

--- a/solution.py
+++ b/solution.py
@@ -22,7 +22,9 @@
 def gather_in_order(shard, axes, sequence):
     blocks = shard[None]
     for k in sequence:
-        blocks = lax.all_gather(blocks, axes[k], axis=0, tiled=True)
+        blocks = jnp.concatenate(
+            lax.all_to_all(jnp.stack([blocks] * lax.axis_size(axes[k])), axes[k], 0, 0), axis=0
+        )
     current = [lax.axis_size(axes[k]) for k in reversed(sequence)]
     blocks = blocks.reshape(*current, *shard.shape)
     turned = sorted(range(len(sequence)), key=lambda place: sequence[len(sequence) - 1 - place])

time: 340 us -> 371 us (1.091)
  waiting for transfers between devices: 109 us -> 127 us
  starting transfers between devices: 0.13 us -> 8.72 us
    all_to_all x0 -> x1, waiting for transfers between devices: none -> 92.6 us  [gather_in_order(): lax.all_to_all(jnp.stack([blocks] * lax.axis_size(axes[k])), axes[k], 0, 0)]
    all_gather x1 -> x0, waiting for transfers between devices: 53.7 us -> none  [gather_in_order(): blocks = lax.all_gather(blocks, axes[k], axis=0, tiled=True)]
    all_gather x1, waiting for transfers between devices: 15.5 us -> 0.01 us  [side_by_side(): filled, at, outs = (lax.all_gather(both, axis, axis=dim, tiled=True), 0, [])]
    all_to_all x0 -> x1, blocking collectives: none -> 10.7 us  [gather_in_order(): lax.all_to_all(jnp.stack([blocks] * lax.axis_size(axes[k])), axes[k], 0, 0)]
    all_gather x1 -> x0, blocking collectives: 10.4 us -> none  [gather_in_order(): blocks = lax.all_gather(blocks, axes[k], axis=0, tiled=True)]
    all_to_all x0 -> x1, starting transfers between devices: none -> 8.6 us  [gather_in_order(): lax.all_to_all(jnp.stack([blocks] * lax.axis_size(axes[k])), axes[k], 0, 0)]
    all_gather x1, waiting for transfers between devices: 34 us -> 28 us  [shards(): kv_part = lax.all_gather(keyvals, ('ctx', 'row'), axis=0, tiled=True)]
    convert_element_type x2 -> x1, local copies, waits for them, and re-layouts: 13.2 us -> 9.27 us  [shards(): wide_events = whole.astype(jnp.float32)]
  transfers between devices with their start and end apart: 4 -> 4, of which waited for: 4 -> 3; matrix products, arithmetic and copies ran while one was open for 10% -> 9% of each run, Pallas kernels for 0% -> 0%
where the time goes in v1:
time: 371 us; the launch traced here: 370 us
  waiting for transfers between devices  127 us (34%)
  blocking collectives  102 us (27%)
  other arithmetic  45.8 us (12%)
  local copies, waits for them, and re-layouts  39.5 us (11%)
  matrix products  31.9 us (9%)
  between operations  13.3 us (4%)
  starting transfers between devices  8.72 us (2%)
    all_to_all x1, waiting for transfers between devices, gather_in_order(): lax.all_to_all(jnp.stack([blocks] * lax.axis_size(axes[k])), axes[k], 0, 0)  92.6 us
    all_to_all x1, blocking collectives, sent_to_all(): lax.all_to_all(jnp.broadcast_to(shard[None], (devices, *shard.shape)), ax...  69 us
    all_gather x1, waiting for transfers between devices, shards(): kv_part = lax.all_gather(keyvals, ('ctx', 'row'), axis=0, tiled=True)  28 us
    all_gather x1, blocking collectives, shards(): domain_part = lax.all_gather(domain_ids, ('ctx', 'row'), axis=0, tiled=True)  22.5 us
    dot_general x16, matrix products, compute_block(): jnp.einsum('kgqn,nkd->qkgd', weights, kv_block[:, :, 1, :], preferred_ele...  19.3 us
    squeeze x16, local copies, waits for them, and re-layouts, shards(): lax.scan(scan_step, totals, (kv_blocks, domain_blocks, firsts))  15.6 us
    all_to_all x1, blocking collectives, gather_in_order(): lax.all_to_all(jnp.stack([blocks] * lax.axis_size(axes[k])), axes[k], 0, 0)  10.7 us
    add x16, other arithmetic, block_place(): return looked_up * group_rows + storage % group_rows  10.5 us
  transfers between devices with their start and end apart: 4, of which 3 were waited for; matrix products, arithmetic and copies ran while one was open for 9% of the time, Pallas kernels for 0%

profile of v1, /device:TPU:8, one launch (start us, length us, event | category | flops | bytes accessed | tf_op | source)
XLA Modules:
  0.0 369.6 jit_solution(17799268287294653943)
XLA Ops:
  7.6 10.7 %all_to_all.15 = bf16[2,1,512,256]{3,2,1,0:T(8,128)(2,1)S(1)} all-to-all(bf16[2,1,512,256]{3,2,1,0:T(8,128)(2,1)S(1)} %pad_maximum_fusion.1), channel_id=1, replica_groups=mesh['ctx'=4,'row'=4,'col_0'=2,'col_1'=8] {'col_0'}, dimensions={0} | all-to-all | bytes 1048576 | tf_op jit(solution)/shard_map/all_to_all | solution.py:26
  18.3 2.4 stack.7
  20.6 8.6 %all-to-all-start.1 = ((bf16[8,2,512,256]{3,2,1,0:T(8,128)(2,1)}), bf16[8,2,512,256]{3,2,1,0:T(8,128)(2,1)}, u32[]{:S(2)}, u32[]{:S(2)}) async-start(bf16[8,2,512,256]{3,2,1,0:T(8,128)(2,1)} %stack.7), calls=%async_computation.1 | async-start | bytes 8388608 | tf_op jit(solution)/shard_map/all_to_all | solution.py:26
  29.3 1.4 constant_dynamic-slice_fusion.1
  32.0 92.6 %all-to-all-done.1 = bf16[8,2,512,256]{3,2,1,0:T(8,128)(2,1)} async-done(((bf16[8,2,512,256]{3,2,1,0:T(8,128)(2,1)}), bf16[8,2,512,256]{3,2,1,0:T(8,128)(2,1)}, u32[]{:S(2)}, u32[]{:S(2)}) %all-to-all-start.1) | async-done | bytes 4194336 | tf_op jit(solution)/shard_map/all_to_all | solution.py:26
  124.7 6.3 %copy_convert_fusion = f32[8,2,512,256]{3,2,0,1:T(8,128)} fusion(bf16[8,2,512,256]{3,2,1,0:T(8,128)(2,1)} %all-to-all-done.1), kind=kLoop, calls=%fused_computation.39 | loop fusion | flops 2097152 | bytes 12582912 | tf_op jit(solution)/shard_map/convert_element_type | solution.py:76
  131.0 9.3 %copy.27 = f32[512,16,256]{0,2,1:T(8,128)} copy(f32[512,16,256]{2,0,1:T(8,128)} %bitcast.96) | data formatting | bytes 16777216 | tf_op jit(solution)/shard_map/convert_element_type | solution.py:76
  140.3 3.1 multiply_reduce_fusion
  143.4 6.5 %fusion.20 = bf16[512,4096]{0,1:T(8,128)(2,1)} fusion(f32[512,16,256]{0,2,1:T(8,128)} %copy.27, f32[512]{0:T(512)S(1)} %add_rsqrt_fusion), kind=kLoop, calls=%fused_computation.37 | loop fusion | flops 4194304 | bytes 12584960 | tf_op jit(solution)/shard_map/convert_element_type | solution.py:80
  149.9 4.2 %fusion.25 = bf16[512,256]{0,1:T(8,128)(2,1)S(1)} fusion(bf16[512,4096]{0,1:T(8,128)(2,1)} %fusion.20, bf16[4096,512]{1,0:T(8,128)(2,1)} %all-gather.5.cloned.1.call-done), kind=kOutput, calls=%fused_computation.44 | convolution fusion | flops 1073872896 | bytes 6553600 | tf_op jit(solution)/shard_map/dot_general | solution.py:87
  155.0 22.5 %all-gather = s32[16,1,512]{2,1,0:T(1,128)S(1)} all-gather(s32[1,1,512]{2,1,0:T(1,128)S(1)} %bitcast.107), channel_id=1, replica_groups=mesh['ctx'=4,'row'=4,'col_0'=2,'col_1'=8] {'ctx','row'}, dimensions={0}, use_global_device_ids=true | all-gather | bytes 34816 | tf_op jit(solution)/shard_map/all_gather | solution.py:123
  177.7 4.2 %fusion.28 = bf16[512,256]{0,1:T(8,128)(2,1)S(1)} fusion(bf16[512,4096]{0,1:T(8,128)(2,1)} %fusion.20, bf16[4096,512]{1,0:T(8,128)(2,1)} %all-gather.5.cloned.1.call-done), kind=kOutput, calls=%fused_computation.45 | convolution fusion | flops 1073872896 | bytes 6553600 | tf_op jit(solution)/shard_map/dot_general | solution.py:86
  182.1 28.0 %all-gather.7.cloned.1.call-done = bf16[8192,1,2,128]{3,0,2,1:T(8,128)(2,1)} async-done(((bf16[512,1,2,128]{3,0,2,1:T(8,128)(2,1)}), bf16[8192,1,2,128]{3,0,2,1:T(8,128)(2,1)}) %all-gather.7.cloned.1.call-update) | async-done | bytes 4194320 | tf_op jit(solution)/shard_map/all_gather | solution.py:122
  210.1 72.2 %while.13 = (s32[]{:T(128)}, f32[512,1,2,128]{0,3,2,1:T(8,128)S(1)}, bf16[16,512,1,2,128]{4,1,0,3,2:T(8,128)(2,1)}, s32[16]{0:T(128)S(1)}, s32[4]{0:T(128)S(1)},...) while((s32[]{:T(128)}, ...), condition=%wide.region_4.5_spmd.clone, body=%wide.region_2.4_spmd.clone.sunk | while | flops 274747904 | bytes 4743363 | solution.py:133
  213.4 1.2 fusion.45
  222.4 1.2 fusion.45
  226.9 1.2 fusion.45
  240.5 1.2 fusion.45
  245.0 1.2 fusion.45
  249.5 1.2 fusion.45
  258.5 1.2 fusion.45
  283.2 69.0 %all_to_all.16 = bf16[4,1024,256]{2,1,0:T(8,128)(2,1)S(1)} all-to-all(bf16[4,1024,256]{2,1,0:T(8,128)(2,1)S(1)} %broadcast_in_dim.70), channel_id=1, replica_groups=mesh['ctx'=4,'row'=4,'col_0'=2,'col_1'=8] {'row'}, dimensions={0} | all-to-all | bytes 4194304 | tf_op jit(solution)/shard_map/all_to_all | solution.py:49
  352.2 6.7 %all-gather.9.cloned.1.call-done = bf16[512,4096]{0,1:T(8,128)(2,1)} async-done(((bf16[512,256]{0,1:T(8,128)(2,1)}), bf16[512,4096]{0,1:T(8,128)(2,1)}) %all-gather.9.cloned.1.call-update) | async-done | bytes 4194320 | tf_op jit(solution)/shard_map/all_gather | solution.py:136
  358.9 4.2 %convolution_convert_fusion = bf16[512,256]{1,0:T(8,128)(2,1)} fusion(bf16[512,4096]{0,1:T(8,128)(2,1)} %all-gather.9.cloned.1.call-done, bf16[4096,256]{1,0:T(8,128)(2,1)S(1)} %bitcast.98), kind=kOutput, calls=%fused_computation.46 | convolution fusion | flops 1073872896 | bytes 6553600 | tf_op jit(solution)/shard_map/dot_general | solution.py:138
  (152 shorter events, 67.3 us)
Async XLA Ops:
  20.6 10.2 %copy-start.1 = (bf16[1024,256]{1,0:T(8,128)(2,1)S(1)}, bf16[1024,256]{1,0:T(8,128)(2,1)}, u32[]{:S(2)}) copy-start(bf16[1024,256]{1,0:T(8,128)(2,1)} %param.12) | copy-start | bytes 1572868
  20.6 104.0 %all-to-all-start.1 = ((bf16[8,2,512,256]{3,2,1,0:T(8,128)(2,1)}), bf16[8,2,512,256]{3,2,1,0:T(8,128)(2,1)}, u32[]{:S(2)}, u32[]{:S(2)}) async-start(bf16[8,2,512,256]{3,2,1,0:T(8,128)(2,1)} %stack.7), calls=%async_computation.1 | async-start | bytes 8388608 | tf_op jit(solution)/shard_map/all_to_all | solution.py:26
  29.2 120.7 %all-gather.5.cloned.1.call-start = ((), (), s32[]{:S(2)}) async-start(), calls=%async_computation.3 | async-start | bytes 5242880 | tf_op jit(solution)/shard_map/all_gather | solution.py:40
  32.0 178.1 %all-gather.7.cloned.1.call-start = ((), (), s32[]{:S(2)}) async-start(), calls=%async_computation.4 | async-start | bytes 4456448 | tf_op jit(solution)/shard_map/all_gather | solution.py:122
  149.9 5.1 %copy-start.2 = (s32[512]{0:T(512)S(1)}, s32[512]{0:T(512)}, u32[]{:S(2)}) copy-start(s32[512]{0:T(512)} %param.10) | copy-start | bytes 6148
  149.9 27.7 %copy-start.3 = (s32[4]{0:T(128)S(1)}, s32[4]{0:T(128)}, u32[]{:S(2)}) copy-start(s32[4]{0:T(128)} %param.11) | copy-start | bytes 52
  155.0 203.9 %all-gather.9.cloned.1.call-start = ((), (), s32[]{:S(2)}) async-start(), calls=%async_computation.5 | async-start | bytes 4456448 | tf_op jit(solution)/shard_map/all_gather | solution.py:136
  177.7 32.4 %copy-start.4 = (f32[2]{0:T(128)S(1)}, f32[2]{0:T(128)}, u32[]{:S(2)}) copy-start(f32[2]{0:T(128)} %param.14) | copy-start | bytes 28
  210.1 73.0 %copy-start = (bf16[1024,256]{1,0:T(8,128)(2,1)S(1)}, bf16[1024,256]{1,0:T(8,128)(2,1)}, u32[]{:S(2)}) copy-start(bf16[1024,256]{1,0:T(8,128)(2,1)} %param.15) | copy-start | bytes 1572868
Sparse Core Ops, SparseCore 0:
  32.1 42.5 all-gather.4
  155.1 54.9 all-gather.6
  283.2 75.6 all-gather.8
